TPU v7x, 32 devices: a whole 2x2x4 slice. The times are simulated.
32 devices in a mesh: rows: 8 (over y, x, core), chan: 4 (over z).
Axes of the slice: x: 2, y: 2, z: 4, core: 2. Of those that a mesh axis runs over, the one named last changes fastest.
Arguments:
- latents: bfloat16 [512, 4, 8, 128], P('chan', None, 'rows'), may hold values from -20 to 20
- cache_one: bfloat16 [512, 2, 8, 128], P('chan', None, 'rows'), may hold values from -4 to 4
- cache_two: bfloat16 [512, 2, 8, 128], P('chan', None, 'rows'), may hold values from -4 to 4
- gain_one: float32 [512], P('chan'), may hold values from 0.25 to 1.75
- bias_one: float32 [512], P('chan'), may hold values from -0.8 to 0.8
- weight_one: bfloat16 [3, 3, 3, 512, 512], P(None, None, None, None, 'chan'), may hold values from -0.0546875 to 0.0546875
- gain_two: float32 [512], P('chan'), may hold values from 0.25 to 1.75
- bias_two: float32 [512], P('chan'), may hold values from -0.8 to 0.8
- weight_two: bfloat16 [3, 3, 3, 512, 512], P(None, None, None, 'chan'), may hold values from -0.0625 to 0.0625
Outputs:
- upsampled: float32 [512, 4, 16, 256], P('chan', None, 'rows')
All inputs are finite; a program needn't handle non-finite values.
Results may differ from a plain program's by a relative error of at most 0.0022.
Values may be sent and summed in bfloat16 or wider, within the bound.
A program may use at most 64 MiB of HBM per device.

v0:
```python
import jax
import jax.numpy as jnp
from jax import lax
from jax.sharding import PartitionSpec as P

CHANNELS = 512
GROUPS = 32
epsilon = 1e-06


def padded(block, sides, width):
    for axis, dim in sides:
        count = lax.axis_size(axis)
        forward = [(i, i + 1) for i in range(count - 1)]
        backward = [(target, source) for source, target in forward]
        low = lax.ppermute(
            lax.slice_in_dim(block, block.shape[dim] - width, None, axis=dim), axis, forward
        )
        high = lax.ppermute(lax.slice_in_dim(block, 0, width, axis=dim), axis, backward)
        block = jnp.concatenate([low, block, high], axis=dim)
    return block


def group_silu(values, gain, bias):
    group_size = CHANNELS // GROUPS
    grouped = values.reshape(values.shape[0] // group_size, -1)
    sums, squares = lax.psum((jnp.sum(grouped, axis=1), jnp.sum(grouped * grouped, axis=1)), "rows")
    members = grouped.shape[1] * lax.axis_size("rows")
    average = sums / members
    spread = squares / members - average * average
    normed = ((grouped - average[:, None]) * lax.rsqrt(spread + epsilon)[:, None]).reshape(
        values.shape
    )
    scaled = normed * gain[:, None, None, None] + bias[:, None, None, None]
    return jax.nn.silu(scaled).astype(jnp.bfloat16)


def pad_rows(frames):
    return padded(frames, (("rows", 2),), 1)


def conv_block(frames, kernel):
    result = lax.conv_general_dilated(
        frames[None],
        kernel,
        (1, 1, 1),
        ((0, 0), (0, 0), (1, 1)),
        dimension_numbers=("NCDHW", "DHWIO", "NCDHW"),
        preferred_element_type=jnp.float32,
    )
    return result[0]


def gathered_conv(frames, kernel):
    initial = jnp.zeros(
        (kernel.shape[4], frames.shape[1] - 2, frames.shape[2] - 2, frames.shape[3]), jnp.float32
    )
    channels = lax.all_gather(frames, "chan", axis=0, tiled=True)
    section = lax.slice_in_dim(kernel, 0, channels.shape[0], axis=3)
    return initial + conv_block(channels, section)


def kernel_columns(kernel):
    return lax.all_to_all(kernel, "chan", split_axis=4, concat_axis=3, tiled=True)


def body(
    latents, cache_one, cache_two, gain_one, bias_one, weight_one, gain_two, bias_two, weight_two
):
    floats = latents.astype(jnp.float32)
    first = group_silu(floats, gain_one, bias_one)
    frames_one = pad_rows(jnp.concatenate([cache_one, first], axis=1))
    middle = gathered_conv(frames_one, weight_one).astype(jnp.bfloat16)
    second = group_silu(middle.astype(jnp.float32), gain_two, bias_two)
    frames_two = pad_rows(jnp.concatenate([cache_two, second], axis=1))
    columns = kernel_columns(weight_two)
    outcome = gathered_conv(frames_two, columns)
    result = floats + outcome
    return jnp.repeat(jnp.repeat(result, 2, axis=2), 2, axis=3)


def solution(mesh):
    return jax.shard_map(
        body,
        mesh=mesh,
        in_specs=(
            P("chan", None, "rows", None),
            P("chan", None, "rows", None),
            P("chan", None, "rows", None),
            P("chan"),
            P("chan"),
            P(None, None, None, None, "chan"),
            P("chan"),
            P("chan"),
            P(None, None, None, "chan", None),
        ),
        out_specs=P("chan", None, "rows", None),
        check_vma=False,
    )
```

profile of v0, /device:TPU:0, one launch (start us, length us, event | category | flops | bytes accessed | tf_op | source)
XLA Modules:
  0.0 272.5 jit_solution(15219196407137967923)
XLA Ops:
  8.1 15.6 %all-reduce.1 = (f32[8]{0:T(128)S(1)}, f32[8]{0:T(128)}) all-reduce(f32[8]{0:T(128)S(1)} %reduce_sum.54, f32[8]{0:T(128)S(1)} %reduce_sum.51), channel_id=1, replica_groups=mesh['rows'=8,'chan'=4] {'rows'}, use_global_device_ids=true, to_apply=%region_5.6 | all-reduce | flops 16 | bytes 128 | tf_op jit(solution)/shard_map/psum | solution.py:27
  28.0 3.0 %collective-permute-start = (bf16[128,6,1,128]{3,0,2,1:T(8,128)(2,1)S(1)}, bf16[128,6,1,128]{3,0,2,1:T(8,128)(2,1)S(1)}, u32[]{:S(2)}, u32[]{:S(2)}) collective-permute-start(bf16[128,6,1,128]{3,0,2,1:T(8,128)(2,1)S(1)} %pad_maximum_fusion.2), channel_id=1, source_target_pairs={{0,4},{4,8},{8,12},{12,16},{16,20},{20,24},{24,28},{1,5},{5,9},{9,... | collective-permute-start | bytes 589832 | tf_op jit(solution)/shard_map/ppermute | solution.py:16
  33.0 8.1 %copy.53 = bf16[3,3,3,128,512]{3,2,1,0,4:T(4,128)(2,1)} copy(bf16[3,3,3,128,512]{4,3,2,1,0:T(8,128)(2,1)} %param.17) | data formatting | bytes 7077888 | tf_op args[8]
  41.1 5.0 %all-to-all-start = ((bf16[3,3,3,128,512]{3,2,1,0,4:T(4,128)(2,1)}), bf16[3,3,3,128,512]{3,2,1,0,4:T(4,128)(2,1)}, u32[]{:S(2)}, u32[]{:S(2)}) async-start(bf16[3,3,3,128,512]{3,2,1,0,4:T(4,128)(2,1)} %copy.53), calls=%async_computation | async-start | bytes 9437184 | tf_op jit(solution)/shard_map/all_to_all | solution.py:64
  46.2 84.4 %all-gather.3.cloned.1.call-done = bf16[512,6,3,128]{3,0,2,1:T(8,128)(2,1)} async-done(((bf16[128,6,3,128]{3,0,2,1:T(8,128)(2,1)}), bf16[512,6,3,128]{3,0,2,1:T(8,128)(2,1)}) %all-gather.3.cloned.1.call-update) | async-done | bytes 2359312 | tf_op jit(solution)/shard_map/all_gather | solution.py:58
  130.6 4.3 %copy.61 = bf16[512,6,3,1,128]{0,4,2,1,3:T(8,128)(2,1)} copy(bf16[512,6,3,1,128]{4,0,2,1,3:T(8,128)(2,1)} %bitcast.64) | data formatting | bytes 4718592
  134.9 4.1 %pad.clone = bf16[512,6,3,1,136]{0,4,2,1,3:T(8,128)(2,1)} pad(bf16[512,6,3,1,128]{0,4,2,1,3:T(8,128)(2,1)} %copy.61, bf16[]{:T(256)} %constant.17), padding=0_0x0_0x0_0x0_0x1_7 | pad | bytes 4866050 | tf_op jit(solution)/shard_map/broadcast_in_dim | solution.py:44
  139.0 5.0 %reshape.105 = bf16[512,6,3,1,8,17]{0,5,4,2,1,3:T(8,128)(2,1)} reshape(bf16[512,6,3,1,136]{0,4,2,1,3:T(8,128)(2,1)} %pad.clone) | data formatting | bytes 5013504 | tf_op jit(solution)/shard_map/conv_general_dilated | solution.py:43
  144.0 3.1 %copy.46 = bf16[512,6,3,1,8,17]{0,4,5,2,1,3:T(8,128)(2,1)S(1)} copy(bf16[512,6,3,1,8,17]{0,5,4,2,1,3:T(8,128)(2,1)} %reshape.105) | data formatting | bytes 5013504 | tf_op jit(solution)/shard_map/conv_general_dilated | solution.py:43
  147.1 4.7 %fusion.27 = (f32[128]{0:T(128)S(1)}, f32[128]{0:T(128)S(1)}, bf16[4,1,8,17,128]{4,2,3,1,0:T(8,128)(2,1)}) fusion(pred[8,17]{0,1:T(8,128)(4,1)S(1)} %copy-done.3, bf16[3,3,3,512,128]{4,3,2,1,0:T(8,128)(2,1)S(1)} %copy-done, bf16[512,6,3,1,7,2]{0,4,5,2,1,3:T(8,128)(2,1)S(1)} %slice.4, bf16[512,6,3,1,8,17]{0,4,5,2,1,3:T(8,128)(2,1)S(1)} %copy.46), kind=kOutput, calls=%fused_computation.28 | convolution fusion | flops 1934147328 | bytes 6444168 | tf_op jit(solution)/shard_map/conv_general_dilated | solution.py:43
  153.7 15.1 %all-reduce = (f32[8]{0:T(128)S(1)}, f32[8]{0:T(128)}) all-reduce(f32[8]{0:T(128)S(1)} %reduce_sum.75, f32[8]{0:T(128)S(1)} %reduce_sum.72), channel_id=1, replica_groups=mesh['rows'=8,'chan'=4] {'rows'}, use_global_device_ids=true, to_apply=%region_11.12 | all-reduce | flops 16 | bytes 128 | tf_op jit(solution)/shard_map/psum | solution.py:27
  176.4 3.2 %collective-permute-start.2 = (bf16[128,6,1,128]{3,0,2,1:T(8,128)(2,1)S(1)}, bf16[128,6,1,128]{3,0,2,1:T(8,128)(2,1)S(1)}, u32[]{:S(2)}, u32[]{:S(2)}) collective-permute-start(bf16[128,6,1,128]{3,0,2,1:T(8,128)(2,1)S(1)} %pad_maximum_fusion.3), channel_id=1, source_target_pairs={{0,4},{4,8},{8,12},{12,16},{16,20},{20,24},{24,28},{1,5},{5,9},{9,... | collective-permute-start | bytes 589832 | tf_op jit(solution)/shard_map/ppermute | solution.py:16
  182.2 5.5 %all-to-all-done = bf16[3,3,3,128,512]{3,2,1,0,4:T(4,128)(2,1)} async-done(((bf16[3,3,3,128,512]{3,2,1,0,4:T(4,128)(2,1)}), bf16[3,3,3,128,512]{3,2,1,0,4:T(4,128)(2,1)}, u32[]{:S(2)}, u32[]{:S(2)}) %all-to-all-start) | async-done | bytes 3538976 | tf_op jit(solution)/shard_map/all_to_all | solution.py:64
  187.7 8.1 %copy.54 = bf16[3,3,3,128,4,128]{5,3,4,2,1,0:T(8,128)(2,1)} copy(bf16[3,3,3,128,4,128]{3,2,1,0,5,4:T(4,128)(2,1)} %bitcast.7) | data formatting | bytes 7077888 | tf_op jit(solution)/shard_map/all_to_all | solution.py:64
  195.7 36.8 %all-gather.5.cloned.1.call-done = bf16[512,6,3,128]{3,0,2,1:T(8,128)(2,1)} async-done(((bf16[128,6,3,128]{3,0,2,1:T(8,128)(2,1)}), bf16[512,6,3,128]{3,0,2,1:T(8,128)(2,1)}) %all-gather.5.cloned.1.call-update) | async-done | bytes 2359312 | tf_op jit(solution)/shard_map/all_gather | solution.py:58
  232.5 4.3 %copy.62 = bf16[512,6,3,1,128]{0,4,2,1,3:T(8,128)(2,1)} copy(bf16[512,6,3,1,128]{4,0,2,1,3:T(8,128)(2,1)} %bitcast.65) | data formatting | bytes 4718592
  236.8 4.1 %pad.2.clone = bf16[512,6,3,1,136]{0,4,2,1,3:T(8,128)(2,1)} pad(bf16[512,6,3,1,128]{0,4,2,1,3:T(8,128)(2,1)} %copy.62, bf16[]{:T(256)} %constant.17), padding=0_0x0_0x0_0x0_0x1_7 | pad | bytes 4866050 | tf_op jit(solution)/shard_map/broadcast_in_dim | solution.py:44
  240.9 5.0 %reshape.114 = bf16[512,6,3,1,8,17]{0,5,4,2,1,3:T(8,128)(2,1)} reshape(bf16[512,6,3,1,136]{0,4,2,1,3:T(8,128)(2,1)} %pad.2.clone) | data formatting | bytes 5013504 | tf_op jit(solution)/shard_map/conv_general_dilated | solution.py:43
  245.9 3.2 %copy.52 = bf16[512,6,3,1,8,17]{0,4,5,2,1,3:T(8,128)(2,1)S(1)} copy(bf16[512,6,3,1,8,17]{0,5,4,2,1,3:T(8,128)(2,1)} %reshape.114) | data formatting | bytes 5013504 | tf_op jit(solution)/shard_map/conv_general_dilated | solution.py:43
  249.2 4.0 %fusion.18 = f32[4,1,8,17,128]{4,2,3,1,0:T(8,128)S(1)} fusion(bf16[3,3,3,512,128]{4,3,2,1,0:T(8,128)(2,1)S(1)} %bitcast.63, bf16[512,6,3,1,7,2]{0,4,5,2,1,3:T(8,128)(2,1)S(1)} %slice.6, bf16[512,6,3,1,8,17]{0,4,5,2,1,3:T(8,128)(2,1)S(1)} %copy.52, pred[8,17]{0,1:T(8,128)(4,1)S(1)} %copy-done.4), kind=kOutput, calls=%fused_computation.17 | convolution fusion | flops 1933660160 | bytes 6582408 | tf_op jit(solution)/shard_map/conv_general_dilated | solution.py:43
  257.5 1.8 copy.57
  259.3 1.9 broadcast_in_dim.24
  261.2 2.0 copy.58
  263.3 2.4 broadcast_in_dim.26
  (56 shorter events, 24.2 us)
Async XLA Ops:
  6.5 140.6 %copy-start = (bf16[3,3,3,512,128]{4,3,2,1,0:T(8,128)(2,1)S(1)}, bf16[3,3,3,512,128]{4,3,2,1,0:T(8,128)(2,1)}, u32[]{:S(2)}) copy-start(bf16[3,3,3,512,128]{4,3,2,1,0:T(8,128)(2,1)} %param.14) | copy-start | bytes 10616836
  6.5 124.1 %all-gather.3.cloned.1.call-start = ((), (), s32[]{:S(2)}) async-start(), calls=%async_computation.1 | async-start | bytes 2949120 | tf_op jit(solution)/shard_map/all_gather | solution.py:58
  26.7 4.4 %collective-permute-start.1 = (bf16[128,6,1,128]{3,0,2,1:T(8,128)(2,1)S(1)}, bf16[128,6,1,128]{3,0,2,1:T(8,128)(2,1)S(1)}, u32[]{:S(2)}, u32[]{:S(2)}) collective-permute-start(bf16[128,6,1,128]{3,0,2,1:T(8,128)(2,1)S(1)} %pad_maximum_fusion.2), channel_id=1, source_target_pairs={{4,0},{8,4},{12,8},{16,12},{20,16},{24,20},{28,24},{5,1},{9,5},{13... | collective-permute-start | bytes 589832 | tf_op jit(solution)/shard_map/ppermute | solution.py:19
  28.0 4.1 %collective-permute-start = (bf16[128,6,1,128]{3,0,2,1:T(8,128)(2,1)S(1)}, bf16[128,6,1,128]{3,0,2,1:T(8,128)(2,1)S(1)}, u32[]{:S(2)}, u32[]{:S(2)}) collective-permute-start(bf16[128,6,1,128]{3,0,2,1:T(8,128)(2,1)S(1)} %pad_maximum_fusion.2), channel_id=1, source_target_pairs={{0,4},{4,8},{8,12},{12,16},{16,20},{20,24},{24,28},{1,5},{5,9},{9,... | collective-permute-start | bytes 589832 | tf_op jit(solution)/shard_map/ppermute | solution.py:16
  41.1 146.5 %all-to-all-start = ((bf16[3,3,3,128,512]{3,2,1,0,4:T(4,128)(2,1)}), bf16[3,3,3,128,512]{3,2,1,0,4:T(4,128)(2,1)}, u32[]{:S(2)}, u32[]{:S(2)}) async-start(bf16[3,3,3,128,512]{3,2,1,0,4:T(4,128)(2,1)} %copy.53), calls=%async_computation | async-start | bytes 9437184 | tf_op jit(solution)/shard_map/all_to_all | solution.py:64
  46.1 186.4 %all-gather.5.cloned.1.call-start = ((), (), s32[]{:S(2)}) async-start(), calls=%async_computation.2 | async-start | bytes 2949120 | tf_op jit(solution)/shard_map/all_gather | solution.py:58
  144.0 3.2 %copy-start.3 = (pred[8,17]{0,1:T(8,128)(4,1)S(1)}, pred[8,17]{0,1:T(8,128)(4,1)}, u32[]{:S(2)}) copy-start(pred[8,17]{0,1:T(8,128)(4,1)} %constant.27) | copy-start | bytes 412
  147.1 26.0 %copy-start.2 = (f32[128]{0:T(128)S(1)}, f32[128]{0:T(128)}, u32[]{:S(2)}) copy-start(f32[128]{0:T(128)} %param.16) | copy-start | bytes 1540
  175.1 4.5 %collective-permute-start.3 = (bf16[128,6,1,128]{3,0,2,1:T(8,128)(2,1)S(1)}, bf16[128,6,1,128]{3,0,2,1:T(8,128)(2,1)S(1)}, u32[]{:S(2)}, u32[]{:S(2)}) collective-permute-start(bf16[128,6,1,128]{3,0,2,1:T(8,128)(2,1)S(1)} %pad_maximum_fusion.3), channel_id=1, source_target_pairs={{4,0},{8,4},{12,8},{16,12},{20,16},{24,20},{28,24},{5,1},{9,5},{13... | collective-permute-start | bytes 589832 | tf_op jit(solution)/shard_map/ppermute | solution.py:19
  176.4 4.1 %collective-permute-start.2 = (bf16[128,6,1,128]{3,0,2,1:T(8,128)(2,1)S(1)}, bf16[128,6,1,128]{3,0,2,1:T(8,128)(2,1)S(1)}, u32[]{:S(2)}, u32[]{:S(2)}) collective-permute-start(bf16[128,6,1,128]{3,0,2,1:T(8,128)(2,1)S(1)} %pad_maximum_fusion.3), channel_id=1, source_target_pairs={{0,4},{4,8},{8,12},{12,16},{16,20},{20,24},{24,28},{1,5},{5,9},{9,... | collective-permute-start | bytes 589832 | tf_op jit(solution)/shard_map/ppermute | solution.py:16
  245.9 3.3 %copy-start.1 = (bf16[3,3,3,128,4,128]{5,3,4,2,1,0:T(8,128)(2,1)S(1)}, bf16[3,3,3,128,4,128]{5,3,4,2,1,0:T(8,128)(2,1)}, u32[]{:S(2)}) copy-start(bf16[3,3,3,128,4,128]{5,3,4,2,1,0:T(8,128)(2,1)} %copy.54) | copy-start | bytes 10616836
  245.9 3.3 %copy-start.4 = (pred[8,17]{0,1:T(8,128)(4,1)S(1)}, pred[8,17]{0,1:T(8,128)(4,1)}, u32[]{:S(2)}) copy-start(pred[8,17]{0,1:T(8,128)(4,1)} %constant.27) | copy-start | bytes 412
Sparse Core Ops, SparseCore 0:
  33.1 97.4 all-gather.2
  182.3 50.1 all-gather.4
where the time goes:
time: 274 us; the launch traced here: 272 us
  waiting for transfers between devices  129 us (47%)
  local copies, waits for them, and re-layouts  66.6 us (24%)
  blocking collectives  30.7 us (11%)
  starting transfers between devices  13.9 us (5%)
  between operations  13.6 us (5%)
  other arithmetic  10.4 us (4%)
  matrix products  8.76 us (3%)
    all_gather x2, waiting for transfers between devices, gathered_conv(): channels = lax.all_gather(frames, 'chan', axis=0, tiled=True)  121 us
    psum x2, blocking collectives, group_silu(): lax.psum((jnp.sum(grouped, axis=1), jnp.sum(grouped * grouped, axis=1)),...  30.7 us
    unnamed x17, local copies, waits for them, and re-layouts  22.4 us
    conv_general_dilated x8, local copies, waits for them, and re-layouts, conv_block(): lax.conv_general_dilated(frames[None], kernel, (1, 1, 1), ((0, 0), (0, 0)...  17.2 us
    conv_general_dilated x2, matrix products, conv_block(): lax.conv_general_dilated(frames[None], kernel, (1, 1, 1), ((0, 0), (0, 0)...  8.76 us
    broadcast_in_dim x2, local copies, waits for them, and re-layouts, conv_block(): frames[None]  8.19 us
    all_to_all x1, local copies, waits for them, and re-layouts, kernel_columns(): lax.all_to_all(kernel, 'chan', split_axis=4, concat_axis=3, tiled=True)  8.07 us
    broadcast_in_dim x3, local copies, waits for them, and re-layouts, body(): return jnp.repeat(jnp.repeat(result, 2, axis=2), 2, axis=3)  6.32 us
  transfers between devices with their start and end apart: 7, of which 5 were waited for; matrix products, arithmetic and copies ran while one was open for 17% of the time, Pallas kernels for 0%

commit v1 on v0

--- a/solution.py
+++ b/solution.py
@@ -61,7 +61,10 @@
 
 
 def kernel_columns(kernel):
-    return lax.all_to_all(kernel, "chan", split_axis=4, concat_axis=3, tiled=True)
+    return jnp.concatenate(
+        lax.all_to_all(jnp.stack(jnp.split(kernel, lax.axis_size("chan"), axis=4)), "chan", 0, 0),
+        axis=3,
+    )
 
 
 def body(

time: 274 us -> 288 us (1.051)
  waiting for transfers between devices: 129 us -> 153 us
  local copies, waits for them, and re-layouts: 66.6 us -> 57.1 us
    all_gather x2, waiting for transfers between devices: 121 us -> 151 us  [gathered_conv(): channels = lax.all_gather(frames, 'chan', axis=0, tiled=True)]
    unnamed x17 -> x16, local copies, waits for them, and re-layouts: 22.4 us -> 14.4 us
    all_to_all x1 -> x0, local copies, waits for them, and re-layouts: 8.07 us -> none  [kernel_columns(): lax.all_to_all(kernel, 'chan', split_axis=4, concat_axis=3, tiled=True)]
    all_to_all x1, waiting for transfers between devices: 5.46 us -> 0.01 us  [kernel_columns(): lax.all_to_all(jnp.stack(jnp.split(kernel, lax.axis_size('chan'), axis=4)...]
    reshape x0 -> x1, local copies, waits for them, and re-layouts: none -> 4.29 us  [kernel_columns(): jnp.concatenate(lax.all_to_all(jnp.stack(jnp.split(kernel, lax.axis_size(...]
  transfers between devices with their start and end apart: 7 -> 7, of which waited for: 5 -> 4; matrix products, arithmetic and copies ran while one was open for 17% -> 14% of each run, Pallas kernels for 0% -> 0%
where the time goes in v1:
time: 288 us; the launch traced here: 287 us
  waiting for transfers between devices  153 us (53%)
  local copies, waits for them, and re-layouts  57.1 us (20%)
  blocking collectives  28 us (10%)
  starting transfers between devices  13.7 us (5%)
  between operations  13.6 us (5%)
  other arithmetic  12.5 us (4%)
  matrix products  8.75 us (3%)
    all_gather x2, waiting for transfers between devices, gathered_conv(): channels = lax.all_gather(frames, 'chan', axis=0, tiled=True)  151 us
    psum x2, blocking collectives, group_silu(): lax.psum((jnp.sum(grouped, axis=1), jnp.sum(grouped * grouped, axis=1)),...  28 us
    conv_general_dilated x8, local copies, waits for them, and re-layouts, conv_block(): lax.conv_general_dilated(frames[None], kernel, (1, 1, 1), ((0, 0), (0, 0)...  17.2 us
    unnamed x16, local copies, waits for them, and re-layouts  14.4 us
    conv_general_dilated x2, matrix products, conv_block(): lax.conv_general_dilated(frames[None], kernel, (1, 1, 1), ((0, 0), (0, 0)...  8.75 us
    broadcast_in_dim x2, local copies, waits for them, and re-layouts, conv_block(): frames[None]  8.28 us
    broadcast_in_dim x3, local copies, waits for them, and re-layouts, body(): return jnp.repeat(jnp.repeat(result, 2, axis=2), 2, axis=3)  6.32 us
    ppermute x2, starting transfers between devices, padded(): lax.ppermute(lax.slice_in_dim(block, block.shape[dim] - width, None, axis...  6.26 us
  transfers between devices with their start and end apart: 7, of which 4 were waited for; matrix products, arithmetic and copies ran while one was open for 14% of the time, Pallas kernels for 0%

profile of v1, /device:TPU:0, one launch (start us, length us, event | category | flops | bytes accessed | tf_op | source)
XLA Modules:
  0.0 286.9 jit_solution(17765885703045261577)
XLA Ops:
  8.1 15.6 %all-reduce.1 = (f32[8]{0:T(128)S(1)}, f32[8]{0:T(128)}) all-reduce(f32[8]{0:T(128)S(1)} %reduce_sum.54, f32[8]{0:T(128)S(1)} %reduce_sum.51), channel_id=1, replica_groups=mesh['rows'=8,'chan'=4] {'rows'}, use_global_device_ids=true, to_apply=%region_5.6 | all-reduce | flops 16 | bytes 128 | tf_op jit(solution)/shard_map/psum | solution.py:27
  28.0 3.0 %collective-permute-start = (bf16[128,6,1,128]{3,0,2,1:T(8,128)(2,1)S(1)}, bf16[128,6,1,128]{3,0,2,1:T(8,128)(2,1)S(1)}, u32[]{:S(2)}, u32[]{:S(2)}) collective-permute-start(bf16[128,6,1,128]{3,0,2,1:T(8,128)(2,1)S(1)} %pad_maximum_fusion.3), channel_id=1, source_target_pairs={{0,4},{4,8},{8,12},{12,16},{16,20},{20,24},{24,28},{1,5},{5,9},{9,... | collective-permute-start | bytes 589832 | tf_op jit(solution)/shard_map/ppermute | solution.py:16
  33.0 2.3 slice_bitcast_fusion.3
  35.3 2.1 pad_maximum_fusion
  37.4 4.9 %all-to-all-start = ((bf16[4,3,3,3,128,128]{5,4,3,2,1,0:T(8,128)(2,1)}), bf16[4,3,3,3,128,128]{5,4,3,2,1,0:T(8,128)(2,1)}, u32[]{:S(2)}, u32[]{:S(2)}) async-start(bf16[4,3,3,3,128,128]{5,4,3,2,1,0:T(8,128)(2,1)} %pad_maximum_fusion), calls=%async_computation | async-start | bytes 7077888 | tf_op jit(solution)/shard_map/all_to_all | solution.py:65
  42.2 100.9 %all-gather.3.cloned.1.call-done = bf16[512,6,3,128]{3,0,2,1:T(8,128)(2,1)} async-done(((bf16[128,6,3,128]{3,0,2,1:T(8,128)(2,1)}), bf16[512,6,3,128]{3,0,2,1:T(8,128)(2,1)}) %all-gather.3.cloned.1.call-update) | async-done | bytes 2359312 | tf_op jit(solution)/shard_map/all_gather | solution.py:58
  143.2 4.3 %copy.44 = bf16[512,6,3,1,128]{0,4,2,1,3:T(8,128)(2,1)} copy(bf16[512,6,3,1,128]{4,0,2,1,3:T(8,128)(2,1)} %bitcast.70) | data formatting | bytes 4718592
  147.4 4.2 %pad.clone = bf16[512,6,3,1,136]{0,4,2,1,3:T(8,128)(2,1)} pad(bf16[512,6,3,1,128]{0,4,2,1,3:T(8,128)(2,1)} %copy.44, bf16[]{:T(256)} %constant.17), padding=0_0x0_0x0_0x0_0x1_7 | pad | bytes 4866050 | tf_op jit(solution)/shard_map/broadcast_in_dim | solution.py:44
  151.6 5.0 %reshape.113 = bf16[512,6,3,1,8,17]{0,5,4,2,1,3:T(8,128)(2,1)} reshape(bf16[512,6,3,1,136]{0,4,2,1,3:T(8,128)(2,1)} %pad.clone) | data formatting | bytes 5013504 | tf_op jit(solution)/shard_map/conv_general_dilated | solution.py:43
  156.7 3.1 %copy.30 = bf16[512,6,3,1,8,17]{0,4,5,2,1,3:T(8,128)(2,1)S(1)} copy(bf16[512,6,3,1,8,17]{0,5,4,2,1,3:T(8,128)(2,1)} %reshape.113) | data formatting | bytes 5013504 | tf_op jit(solution)/shard_map/conv_general_dilated | solution.py:43
  159.8 4.7 %fusion.27 = (f32[128]{0:T(128)S(1)}, f32[128]{0:T(128)S(1)}, bf16[4,1,8,17,128]{4,2,3,1,0:T(8,128)(2,1)}) fusion(pred[8,17]{0,1:T(8,128)(4,1)S(1)} %copy-done.3, bf16[3,3,3,512,128]{4,3,2,1,0:T(8,128)(2,1)S(1)} %copy-done, bf16[512,6,3,1,7,2]{0,4,5,2,1,3:T(8,128)(2,1)S(1)} %slice.4, bf16[512,6,3,1,8,17]{0,4,5,2,1,3:T(8,128)(2,1)S(1)} %copy.30), kind=kOutput, calls=%fused_computation.33 | convolution fusion | flops 1934147328 | bytes 6444168 | tf_op jit(solution)/shard_map/conv_general_dilated | solution.py:43
  166.4 12.4 %all-reduce = (f32[8]{0:T(128)S(1)}, f32[8]{0:T(128)}) all-reduce(f32[8]{0:T(128)S(1)} %reduce_sum.75, f32[8]{0:T(128)S(1)} %reduce_sum.72), channel_id=1, replica_groups=mesh['rows'=8,'chan'=4] {'rows'}, use_global_device_ids=true, to_apply=%region_11.12 | all-reduce | flops 16 | bytes 128 | tf_op jit(solution)/shard_map/psum | solution.py:27
  186.4 3.2 %collective-permute-start.2 = (bf16[128,6,1,128]{3,0,2,1:T(8,128)(2,1)S(1)}, bf16[128,6,1,128]{3,0,2,1:T(8,128)(2,1)S(1)}, u32[]{:S(2)}, u32[]{:S(2)}) collective-permute-start(bf16[128,6,1,128]{3,0,2,1:T(8,128)(2,1)S(1)} %pad_maximum_fusion.4), channel_id=1, source_target_pairs={{0,4},{4,8},{8,12},{12,16},{16,20},{20,24},{24,28},{1,5},{5,9},{9,... | collective-permute-start | bytes 589832 | tf_op jit(solution)/shard_map/ppermute | solution.py:16
  192.2 4.3 %copy.37 = bf16[3,3,3,4,128,128]{5,4,3,2,1,0:T(8,128)(2,1)} copy(bf16[3,3,3,4,128,128]{5,4,2,1,0,3:T(8,128)(2,1)} %bitcast.11) | data formatting | bytes 7077888 | tf_op jit(solution)/shard_map/reshape | solution.py:64
  196.5 50.4 %all-gather.5.cloned.1.call-done = bf16[512,6,3,128]{3,0,2,1:T(8,128)(2,1)} async-done(((bf16[128,6,3,128]{3,0,2,1:T(8,128)(2,1)}), bf16[512,6,3,128]{3,0,2,1:T(8,128)(2,1)}) %all-gather.5.cloned.1.call-update) | async-done | bytes 2359312 | tf_op jit(solution)/shard_map/all_gather | solution.py:58
  246.9 4.3 %copy.45 = bf16[512,6,3,1,128]{0,4,2,1,3:T(8,128)(2,1)} copy(bf16[512,6,3,1,128]{4,0,2,1,3:T(8,128)(2,1)} %bitcast.71) | data formatting | bytes 4718592
  251.2 4.1 %pad.2.clone = bf16[512,6,3,1,136]{0,4,2,1,3:T(8,128)(2,1)} pad(bf16[512,6,3,1,128]{0,4,2,1,3:T(8,128)(2,1)} %copy.45, bf16[]{:T(256)} %constant.17), padding=0_0x0_0x0_0x0_0x1_7 | pad | bytes 4866050 | tf_op jit(solution)/shard_map/broadcast_in_dim | solution.py:44
  255.3 5.0 %reshape.122 = bf16[512,6,3,1,8,17]{0,5,4,2,1,3:T(8,128)(2,1)} reshape(bf16[512,6,3,1,136]{0,4,2,1,3:T(8,128)(2,1)} %pad.2.clone) | data formatting | bytes 5013504 | tf_op jit(solution)/shard_map/conv_general_dilated | solution.py:43
  260.3 3.2 %copy.36 = bf16[512,6,3,1,8,17]{0,4,5,2,1,3:T(8,128)(2,1)S(1)} copy(bf16[512,6,3,1,8,17]{0,5,4,2,1,3:T(8,128)(2,1)} %reshape.122) | data formatting | bytes 5013504 | tf_op jit(solution)/shard_map/conv_general_dilated | solution.py:43
  263.6 4.0 %fusion.18 = f32[4,1,8,17,128]{4,2,3,1,0:T(8,128)S(1)} fusion(bf16[3,3,3,512,128]{4,3,2,1,0:T(8,128)(2,1)S(1)} %bitcast.69, bf16[512,6,3,1,7,2]{0,4,5,2,1,3:T(8,128)(2,1)S(1)} %slice.6, bf16[512,6,3,1,8,17]{0,4,5,2,1,3:T(8,128)(2,1)S(1)} %copy.36, pred[8,17]{0,1:T(8,128)(4,1)S(1)} %copy-done.4), kind=kOutput, calls=%fused_computation.18 | convolution fusion | flops 1933660160 | bytes 6582408 | tf_op jit(solution)/shard_map/conv_general_dilated | solution.py:43
  271.9 1.8 copy.40
  273.7 1.9 broadcast_in_dim.24
  275.6 2.0 copy.41
  277.7 2.4 broadcast_in_dim.26
  (57 shorter events, 24.2 us)
Async XLA Ops:
  6.5 153.3 %copy-start = (bf16[3,3,3,512,128]{4,3,2,1,0:T(8,128)(2,1)S(1)}, bf16[3,3,3,512,128]{4,3,2,1,0:T(8,128)(2,1)}, u32[]{:S(2)}) copy-start(bf16[3,3,3,512,128]{4,3,2,1,0:T(8,128)(2,1)} %param.14) | copy-start | bytes 10616836
  6.5 136.6 %all-gather.3.cloned.1.call-start = ((), (), s32[]{:S(2)}) async-start(), calls=%async_computation.1 | async-start | bytes 2949120 | tf_op jit(solution)/shard_map/all_gather | solution.py:58
  26.7 4.4 %collective-permute-start.1 = (bf16[128,6,1,128]{3,0,2,1:T(8,128)(2,1)S(1)}, bf16[128,6,1,128]{3,0,2,1:T(8,128)(2,1)S(1)}, u32[]{:S(2)}, u32[]{:S(2)}) collective-permute-start(bf16[128,6,1,128]{3,0,2,1:T(8,128)(2,1)S(1)} %pad_maximum_fusion.3), channel_id=1, source_target_pairs={{4,0},{8,4},{12,8},{16,12},{20,16},{24,20},{28,24},{5,1},{9,5},{13... | collective-permute-start | bytes 589832 | tf_op jit(solution)/shard_map/ppermute | solution.py:19
  28.0 4.1 %collective-permute-start = (bf16[128,6,1,128]{3,0,2,1:T(8,128)(2,1)S(1)}, bf16[128,6,1,128]{3,0,2,1:T(8,128)(2,1)S(1)}, u32[]{:S(2)}, u32[]{:S(2)}) collective-permute-start(bf16[128,6,1,128]{3,0,2,1:T(8,128)(2,1)S(1)} %pad_maximum_fusion.3), channel_id=1, source_target_pairs={{0,4},{4,8},{8,12},{12,16},{16,20},{20,24},{24,28},{1,5},{5,9},{9,... | collective-permute-start | bytes 589832 | tf_op jit(solution)/shard_map/ppermute | solution.py:16
  37.4 154.9 %all-to-all-start = ((bf16[4,3,3,3,128,128]{5,4,3,2,1,0:T(8,128)(2,1)}), bf16[4,3,3,3,128,128]{5,4,3,2,1,0:T(8,128)(2,1)}, u32[]{:S(2)}, u32[]{:S(2)}) async-start(bf16[4,3,3,3,128,128]{5,4,3,2,1,0:T(8,128)(2,1)} %pad_maximum_fusion), calls=%async_computation | async-start | bytes 7077888 | tf_op jit(solution)/shard_map/all_to_all | solution.py:65
  42.2 204.7 %all-gather.5.cloned.1.call-start = ((), (), s32[]{:S(2)}) async-start(), calls=%async_computation.2 | async-start | bytes 2949120 | tf_op jit(solution)/shard_map/all_gather | solution.py:58
  156.7 3.2 %copy-start.3 = (pred[8,17]{0,1:T(8,128)(4,1)S(1)}, pred[8,17]{0,1:T(8,128)(4,1)}, u32[]{:S(2)}) copy-start(pred[8,17]{0,1:T(8,128)(4,1)} %constant.27) | copy-start | bytes 412
  159.8 23.3 %copy-start.2 = (f32[128]{0:T(128)S(1)}, f32[128]{0:T(128)}, u32[]{:S(2)}) copy-start(f32[128]{0:T(128)} %param.16) | copy-start | bytes 1540
  185.1 4.5 %collective-permute-start.3 = (bf16[128,6,1,128]{3,0,2,1:T(8,128)(2,1)S(1)}, bf16[128,6,1,128]{3,0,2,1:T(8,128)(2,1)S(1)}, u32[]{:S(2)}, u32[]{:S(2)}) collective-permute-start(bf16[128,6,1,128]{3,0,2,1:T(8,128)(2,1)S(1)} %pad_maximum_fusion.4), channel_id=1, source_target_pairs={{4,0},{8,4},{12,8},{16,12},{20,16},{24,20},{28,24},{5,1},{9,5},{13... | collective-permute-start | bytes 589832 | tf_op jit(solution)/shard_map/ppermute | solution.py:19
  186.4 4.1 %collective-permute-start.2 = (bf16[128,6,1,128]{3,0,2,1:T(8,128)(2,1)S(1)}, bf16[128,6,1,128]{3,0,2,1:T(8,128)(2,1)S(1)}, u32[]{:S(2)}, u32[]{:S(2)}) collective-permute-start(bf16[128,6,1,128]{3,0,2,1:T(8,128)(2,1)S(1)} %pad_maximum_fusion.4), channel_id=1, source_target_pairs={{0,4},{4,8},{8,12},{12,16},{16,20},{20,24},{24,28},{1,5},{5,9},{9,... | collective-permute-start | bytes 589832 | tf_op jit(solution)/shard_map/ppermute | solution.py:16
  260.3 3.3 %copy-start.1 = (bf16[3,3,3,4,128,128]{5,4,3,2,1,0:T(8,128)(2,1)S(1)}, bf16[3,3,3,4,128,128]{5,4,3,2,1,0:T(8,128)(2,1)}, u32[]{:S(2)}) copy-start(bf16[3,3,3,4,128,128]{5,4,3,2,1,0:T(8,128)(2,1)} %copy.37) | copy-start | bytes 10616836
  260.3 3.3 %copy-start.4 = (pred[8,17]{0,1:T(8,128)(4,1)S(1)}, pred[8,17]{0,1:T(8,128)(4,1)}, u32[]{:S(2)}) copy-start(pred[8,17]{0,1:T(8,128)(4,1)} %constant.27) | copy-start | bytes 412
Sparse Core Ops, SparseCore 0:
  33.1 109.9 all-gather.2
  192.4 54.4 all-gather.4
